TPU v7x, 32 devices: a whole 2x2x4 slice. The times are simulated.
32 devices in a mesh: row: 8 (over z, x), col: 4 (over y, core).
Axes of the slice: x: 2, y: 2, z: 4, core: 2. Of those that a mesh axis runs over, the one named last changes fastest.
Arguments:
- vectors: float32 [8, 4096], P(None, ('row', 'col')), may hold values from -6 to 6
- values: float32 [512, 16384], P('row', 'col'), may hold values from -1 to 1
- block_rows: int32 [8, 256], P('row', 'col'), may hold values from 0 to 7
- block_cols: int32 [8, 256], P('row', 'col'), may hold values from 0 to 15
- counts: int32 [8, 4], P('row', 'col'), may hold values from 16 to 64, as said below
Outputs:
- product: float32 [8, 4096], P(None, ('row', 'col'))
Inputs may be any that keep to these rules, and one draw needn't show every extreme that they name: counts[r, c] slots of tile (r, c) hold blocks, the others are unused; some tile uses all 64 slots.
All inputs are finite; a program needn't handle non-finite values.
Results may differ from a plain program's by a relative error of at most 0.0003.
Values sent between devices are 32-bit elements; how exact they have to be, the bound alone decides.
No kernel may reach another device: no remote copies, remote signals or barrier semaphores. Data moves between devices by JAX's collectives and lax.ppermute only.
A program may use at most 64 MiB of HBM per device.

v0:
```python
import jax
import jax.numpy as jnp
from jax import lax
from jax.sharding import PartitionSpec as P

BLK = 64


def tile_terms(blocks, rows, cols, count, row_seg, col_seg):
    highest = lax.Precision.HIGHEST
    slots = blocks.shape[0]
    nvec = row_seg.shape[0]
    row_blocks = row_seg.shape[1] // blocks.shape[1]
    col_blocks = col_seg.shape[1] // blocks.shape[1]
    width = blocks.shape[1]
    live = (jnp.arange(slots, dtype=jnp.int32) < count).astype(jnp.float32)
    row_hits = (rows[:, None] == jnp.arange(row_blocks, dtype=jnp.int32)[None, :]).astype(
        jnp.float32
    ) * live[:, None]
    col_hits = (cols[:, None] == jnp.arange(col_blocks, dtype=jnp.int32)[None, :]).astype(
        jnp.float32
    ) * live[:, None]
    row_parts = row_seg.reshape(nvec, row_blocks, width)
    col_parts = col_seg.reshape(nvec, col_blocks, width)
    col_pick = jnp.take(col_parts, cols, axis=1)
    row_pick = jnp.take(row_parts, rows, axis=1)
    plain = jnp.einsum("kij,vkj->vki", blocks, col_pick, precision=highest)
    turned = jnp.einsum("kji,vkj->vki", blocks, row_pick, precision=highest)
    plain_part = jnp.einsum("kb,vki->vbi", row_hits, plain, precision=highest).reshape(
        nvec, row_blocks * width
    )
    turned_part = jnp.einsum("kb,vki->vbi", col_hits, turned, precision=highest).reshape(
        nvec, col_blocks * width
    )
    return (plain_part, turned_part)


def sum_rows(plain_part):
    return lax.psum_scatter(plain_part, "col", scatter_dimension=1, tiled=True)


def sum_columns(turned_part):
    return lax.psum_scatter(turned_part, "row", scatter_dimension=1, tiled=True)


def per_device(vectors, values, block_rows, block_cols, counts):
    row_seg = lax.all_gather(vectors, "col", axis=1, tiled=True)
    col_seg = lax.all_gather(vectors, "row", axis=1, tiled=True)
    blocks = values.reshape(values.shape[0], BLK, BLK)
    rows = block_rows[0]
    cols = block_cols[0]
    count = counts[0, 0]
    plain_part, turned_part = tile_terms(blocks, rows, cols, count, row_seg, col_seg)
    plain_sum = sum_rows(plain_part)
    turned_sum = sum_columns(turned_part)
    return plain_sum + turned_sum


def solution(mesh):
    in_specs = (
        P(None, ("row", "col")),
        P("row", "col"),
        P("row", "col"),
        P("row", "col"),
        P("row", "col"),
    )
    out_specs = P(None, ("row", "col"))
    return jax.shard_map(
        per_device, mesh=mesh, in_specs=in_specs, out_specs=out_specs, check_vma=False
    )
```

profile of v0, /device:TPU:0, one launch (start us, length us, event | category | flops | bytes accessed | tf_op | source)
XLA Modules:
  0.0 134.8 jit_solution(16836529348863672988)
XLA Ops:
  6.5 0.0 copy-start
  6.5 0.0 reduce-scatter.3.cloned.1.call-start
  6.5 0.7 fusion.20
  7.2 0.7 compare_and_fusion.1
  7.9 2.0 %reshape.91 = f32[64,64,64]{2,1,0:T(8,128)S(1)} reshape(f32[64,4096]{1,0:T(8,128)} %param.6) | data formatting | bytes 2097152 | tf_op jit(solution)/shard_map/reshape | solution.py:49
  9.9 0.0 copy-done
  9.9 0.0 copy-start.1
  9.9 32.4 %all_gather.6 = f32[8,1024]{1,0:T(8,128)S(1)} all-gather(f32[8,128]{1,0:T(8,128)S(1)} %copy-done), channel_id=1, replica_groups=mesh['row'=8,'col'=4] {'row'}, dimensions={1}, use_global_device_ids=true | all-gather | bytes 36864 | tf_op jit(solution)/shard_map/all_gather | solution.py:48
  42.3 0.1 reshape.90
  43.1 0.6 gather_fusion
  43.7 3.4 %convolution_bitcast_fusion.1 = f32[8,64,64]{2,0,1:T(8,128)S(1)} fusion(f32[64,64,64]{2,1,0:T(8,128)S(1)} %reshape.91, f32[64,8,64]{2,1,0:T(8,128)S(1)} %gather_fusion, pred[64]{0:T(512)(128)(4,1)S(1)} %compare_and_fusion.1), kind=kOutput, calls=%fused_computation.3 | convolution fusion | flops 25198592 | bytes 1310784 | tf_op jit(solution)/shard_map/kij,vkj->vki/dot_general | solution.py:27
  47.1 0.0 copy-start.2
  47.2 0.0 copy-done.1
  47.2 0.3 convolution_bitcast_fusion.3
  47.4 0.7 reshape.92
  48.1 0.0 reduce-scatter.3.cloned.1.call-update
  48.1 0.0 reduce-scatter.5.cloned.1.call-start
  48.2 5.2 %all_gather.7 = f32[8,512]{1,0:T(8,128)S(1)} all-gather(f32[8,128]{1,0:T(8,128)S(1)} %copy-done), channel_id=1, replica_groups=mesh['row'=8,'col'=4] {'col'}, dimensions={1}, use_global_device_ids=true | all-gather | bytes 20480 | tf_op jit(solution)/shard_map/all_gather | solution.py:47
  53.4 0.1 reshape.93
  53.5 0.6 gather_fusion.1
  54.1 1.9 %convolution_bitcast_fusion = f32[8,64,64]{2,0,1:T(8,128)S(1)} fusion(f32[64,64,64]{2,1,0:T(8,128)S(1)} %reshape.91, f32[64,8,64]{2,1,0:T(8,128)S(1)} %gather_fusion.1, pred[64]{0:T(512)(128)(4,1)S(1)} %compare_and_fusion), kind=kOutput, calls=%fused_computation.2 | convolution fusion | flops 25198592 | bytes 1310784 | tf_op jit(solution)/shard_map/kji,vkj->vki/dot_general | solution.py:28
  56.1 0.0 copy-done.2
  56.1 0.3 convolution_bitcast_fusion.2
  56.3 0.7 reshape.94
  57.0 0.0 reduce-scatter.5.cloned.1.call-update
  57.0 11.7 %reduce-scatter.3.cloned.1.call-done = f32[8,128]{1,0:T(8,128)} async-done(((f32[8,512]{1,0:T(8,128)}), f32[8,128]{1,0:T(8,128)}) %reduce-scatter.3.cloned.1.call-update) | async-done | bytes 4112 | tf_op jit(solution)/shard_map/reduce_scatter | solution.py:39
  68.7 57.9 %reduce-scatter.5.cloned.1.call-done = f32[8,128]{1,0:T(8,128)} async-done(((f32[8,1024]{1,0:T(8,128)}), f32[8,128]{1,0:T(8,128)}) %reduce-scatter.5.cloned.1.call-update) | async-done | bytes 4112 | tf_op jit(solution)/shard_map/reduce_scatter | solution.py:43
  126.6 1.3 add.57
  (7 shorter events, 0.1 us)
Async XLA Ops:
  6.5 3.3 %copy-start = (f32[8,128]{1,0:T(8,128)S(1)}, f32[8,128]{1,0:T(8,128)}, u32[]{:S(2)}) copy-start(f32[8,128]{1,0:T(8,128)} %param.5) | copy-start | bytes 12292
  6.5 62.2 %reduce-scatter.3.cloned.1.call-start = ((), (), s32[]{:S(2)}) async-start(), calls=%async_computation.2 | async-start | bytes 20480 | tf_op jit(solution)/shard_map/reduce_scatter | solution.py:39
  9.9 37.3 %copy-start.1 = (s32[1,64]{1,0:T(1,128)S(1)}, s32[1,64]{1,0:T(1,128)}, u32[]{:S(2)}) copy-start(s32[1,64]{1,0:T(1,128)} %param.7) | copy-start | bytes 772
  47.1 8.9 %copy-start.2 = (s32[1,64]{1,0:T(1,128)S(1)}, s32[1,64]{1,0:T(1,128)}, u32[]{:S(2)}) copy-start(s32[1,64]{1,0:T(1,128)} %param.8) | copy-start | bytes 772
  48.1 78.5 %reduce-scatter.5.cloned.1.call-start = ((), (), s32[]{:S(2)}) async-start(), calls=%async_computation.3 | async-start | bytes 36864 | tf_op jit(solution)/shard_map/reduce_scatter | solution.py:43
Sparse Core Ops, SparseCore 0:
  48.3 20.4 reduce-scatter.2
  71.9 54.7 reduce-scatter.4
where the time goes:
time: 135 us
  waiting for transfers between devices  69.6 us (52%)
  blocking collectives  37.6 us (28%)
  between operations  14.1 us (10%)
  matrix products  5.88 us (4%)
  local copies, waits for them, and re-layouts  4.82 us (4%)
  other arithmetic  2.63 us (2%)
    reduce_scatter x1, waiting for transfers between devices, sum_columns(): return lax.psum_scatter(turned_part, 'row', scatter_dimension=1, tiled=True)  57.9 us
    all_gather x1, blocking collectives, per_device(): col_seg = lax.all_gather(vectors, 'row', axis=1, tiled=True)  32.4 us
    reduce_scatter x1, waiting for transfers between devices, sum_rows(): return lax.psum_scatter(plain_part, 'col', scatter_dimension=1, tiled=True)  11.7 us
    all_gather x1, blocking collectives, per_device(): row_seg = lax.all_gather(vectors, 'col', axis=1, tiled=True)  5.21 us
    dot_general x1, matrix products, tile_terms(): plain = jnp.einsum('kij,vkj->vki', blocks, col_pick, precision=highest)  3.41 us
  transfers between devices with their start and end apart: 2, of which 2 were waited for; matrix products, arithmetic and copies ran while one was open for 3% of the time, Pallas kernels for 0%

commit v1 on v0

--- a/solution.py
+++ b/solution.py
@@ -45,7 +45,8 @@
 
 def per_device(vectors, values, block_rows, block_cols, counts):
     row_seg = lax.all_gather(vectors, "col", axis=1, tiled=True)
-    col_seg = lax.all_gather(vectors, "row", axis=1, tiled=True)
+    stack = jnp.stack([vectors] * lax.axis_size("row"))
+    col_seg = jnp.concatenate(lax.all_to_all(stack, "row", 0, 0), axis=1)
     blocks = values.reshape(values.shape[0], BLK, BLK)
     rows = block_rows[0]
     cols = block_cols[0]

time: 135 us -> 114 us (0.84)
  blocking collectives: 37.6 us -> 5.34 us
  starting transfers between devices: 0.04 us -> 7.36 us
  waiting for transfers between devices: 69.6 us -> 72.1 us
    all_gather x1 -> x0, blocking collectives: 32.4 us -> none  [per_device(): col_seg = lax.all_gather(vectors, 'row', axis=1, tiled=True)]
    reduce_scatter x1, waiting for transfers between devices: 11.7 us -> 21 us  [sum_rows(): return lax.psum_scatter(plain_part, 'col', scatter_dimension=1, tiled=True)]
    all_to_all x0 -> x1, starting transfers between devices: none -> 7.28 us  [per_device(): col_seg = jnp.concatenate(lax.all_to_all(stack, 'row', 0, 0), axis=1)]
    reduce_scatter x1, waiting for transfers between devices: 57.9 us -> 51.1 us  [sum_columns(): return lax.psum_scatter(turned_part, 'row', scatter_dimension=1, tiled=True)]
    another operation x0 -> x3, local copies, waits for them, and re-layouts: none -> 1.4 us  [the longest x1 1.3 us: per_device(): stack = jnp.stack([vectors] * lax.axis_size('row'))]
  transfers between devices with their start and end apart: 2 -> 3, of which waited for: 2 -> 2; matrix products, arithmetic and copies ran while one was open for 3% -> 11% of each run, Pallas kernels for 0% -> 0%
where the time goes in v1:
time: 114 us
  waiting for transfers between devices  72.1 us (63%)
  between operations  14.2 us (12%)
  starting transfers between devices  7.36 us (6%)
  local copies, waits for them, and re-layouts  6.13 us (5%)
  matrix products  5.87 us (5%)
  blocking collectives  5.34 us (5%)
  other arithmetic  2.63 us (2%)
    reduce_scatter x1, waiting for transfers between devices, sum_columns(): return lax.psum_scatter(turned_part, 'row', scatter_dimension=1, tiled=True)  51.1 us
    reduce_scatter x1, waiting for transfers between devices, sum_rows(): return lax.psum_scatter(plain_part, 'col', scatter_dimension=1, tiled=True)  21 us
    all_to_all x1, starting transfers between devices, per_device(): col_seg = jnp.concatenate(lax.all_to_all(stack, 'row', 0, 0), axis=1)  7.28 us
    all_gather x1, blocking collectives, per_device(): row_seg = lax.all_gather(vectors, 'col', axis=1, tiled=True)  5.34 us
    dot_general x1, matrix products, tile_terms(): plain = jnp.einsum('kij,vkj->vki', blocks, col_pick, precision=highest)  3.41 us
  transfers between devices with their start and end apart: 3, of which 2 were waited for; matrix products, arithmetic and copies ran while one was open for 11% of the time, Pallas kernels for 0%

profile of v1, /device:TPU:0, one launch (start us, length us, event | category | flops | bytes accessed | tf_op | source)
XLA Modules:
  0.0 113.6 jit_solution(4250208358968856334)
XLA Ops:
  6.5 1.3 %stack.2 = f32[8,8,128]{2,1,0:T(8,128)} broadcast(f32[8,128]{1,0:T(8,128)} %param.5), dimensions={1,2} | broadcast | bytes 36864 | tf_op jit(solution)/shard_map/stack | solution.py:48
  7.8 7.3 %all-to-all-start = ((f32[8,8,128]{2,1,0:T(8,128)}), f32[8,8,128]{2,1,0:T(8,128)S(1)}, u32[]{:S(2)}, u32[]{:S(2)}) async-start(f32[8,8,128]{2,1,0:T(8,128)} %stack.2), calls=%async_computation | async-start | bytes 65536 | tf_op jit(solution)/shard_map/all_to_all | solution.py:49
  15.1 0.0 reduce-scatter.5.cloned.1.call-start
  15.2 5.3 %all_gather.3 = f32[8,512]{1,0:T(8,128)S(1)} all-gather(f32[8,128]{1,0:T(8,128)} %param.5), channel_id=1, replica_groups=mesh['row'=8,'col'=4] {'col'}, dimensions={1}, use_global_device_ids=true | all-gather | bytes 20480 | tf_op jit(solution)/shard_map/all_gather | solution.py:47
  20.5 0.7 fusion.21
  21.2 0.7 compare_and_fusion
  21.8 2.0 %reshape.93 = f32[64,64,64]{2,1,0:T(8,128)S(1)} reshape(f32[64,4096]{1,0:T(8,128)} %param.6) | data formatting | bytes 2097152 | tf_op jit(solution)/shard_map/reshape | solution.py:50
  23.8 0.0 copy-start
  24.5 0.1 reshape.95
  24.6 0.6 gather_fusion.1
  25.2 1.9 %convolution_bitcast_fusion = f32[8,64,64]{2,0,1:T(8,128)S(1)} fusion(f32[64,64,64]{2,1,0:T(8,128)S(1)} %reshape.93, f32[64,8,64]{2,1,0:T(8,128)S(1)} %gather_fusion.1, pred[64]{0:T(512)(128)(4,1)S(1)} %compare_and_fusion), kind=kOutput, calls=%fused_computation.2 | convolution fusion | flops 25198592 | bytes 1310784 | tf_op jit(solution)/shard_map/kji,vkj->vki/dot_general | solution.py:28
  27.2 0.0 copy-start.1
  27.2 0.0 copy-done
  27.2 0.3 convolution_bitcast_fusion.2
  27.5 0.7 reshape.96
  28.1 0.0 reduce-scatter.5.cloned.1.call-update
  28.2 0.0 reduce-scatter.3.cloned.1.call-start
  28.3 0.0 all-to-all-done
  28.3 0.1 reshape_reshape.3
  28.4 0.6 gather_fusion
  29.0 3.4 %convolution_bitcast_fusion.1 = f32[8,64,64]{2,0,1:T(8,128)S(1)} fusion(f32[64,64,64]{2,1,0:T(8,128)S(1)} %reshape.93, f32[64,8,64]{2,1,0:T(8,128)S(1)} %gather_fusion, pred[64]{0:T(512)(128)(4,1)S(1)} %compare_and_fusion.1), kind=kOutput, calls=%fused_computation.3 | convolution fusion | flops 25198592 | bytes 1310784 | tf_op jit(solution)/shard_map/kij,vkj->vki/dot_general | solution.py:27
  32.4 0.0 copy-done.1
  32.4 0.3 convolution_bitcast_fusion.3
  32.7 0.7 reshape.94
  33.4 0.0 reduce-scatter.3.cloned.1.call-update
  33.4 51.1 %reduce-scatter.5.cloned.1.call-done = f32[8,128]{1,0:T(8,128)} async-done(((f32[8,1024]{1,0:T(8,128)}), f32[8,128]{1,0:T(8,128)}) %reduce-scatter.5.cloned.1.call-update) | async-done | bytes 4112 | tf_op jit(solution)/shard_map/reduce_scatter | solution.py:43
  84.5 21.0 %reduce-scatter.3.cloned.1.call-done = f32[8,128]{1,0:T(8,128)} async-done(((f32[8,512]{1,0:T(8,128)}), f32[8,128]{1,0:T(8,128)}) %reduce-scatter.3.cloned.1.call-update) | async-done | bytes 4112 | tf_op jit(solution)/shard_map/reduce_scatter | solution.py:39
  105.5 1.3 %add.57 = f32[8,128]{1,0:T(8,128)} add(f32[8,128]{1,0:T(8,128)} %reduce-scatter.3.cloned.1.call-done, f32[8,128]{1,0:T(8,128)} %reduce-scatter.5.cloned.1.call-done) | non-fusion elementwise | flops 1024 | bytes 12288 | tf_op jit(solution)/shard_map/add | solution.py:57
  (8 shorter events, 0.1 us)
Async XLA Ops:
  7.8 20.4 %all-to-all-start = ((f32[8,8,128]{2,1,0:T(8,128)}), f32[8,8,128]{2,1,0:T(8,128)S(1)}, u32[]{:S(2)}, u32[]{:S(2)}) async-start(f32[8,8,128]{2,1,0:T(8,128)} %stack.2), calls=%async_computation | async-start | bytes 65536 | tf_op jit(solution)/shard_map/all_to_all | solution.py:49
  15.1 69.4 %reduce-scatter.5.cloned.1.call-start = ((), (), s32[]{:S(2)}) async-start(), calls=%async_computation.4 | async-start | bytes 36864 | tf_op jit(solution)/shard_map/reduce_scatter | solution.py:43
  23.8 3.3 %copy-start = (s32[1,64]{1,0:T(1,128)S(1)}, s32[1,64]{1,0:T(1,128)}, u32[]{:S(2)}) copy-start(s32[1,64]{1,0:T(1,128)} %param.8) | copy-start | bytes 772
  27.2 5.3 %copy-start.1 = (s32[1,64]{1,0:T(1,128)S(1)}, s32[1,64]{1,0:T(1,128)}, u32[]{:S(2)}) copy-start(s32[1,64]{1,0:T(1,128)} %param.7) | copy-start | bytes 772
  28.2 77.3 %reduce-scatter.3.cloned.1.call-start = ((), (), s32[]{:S(2)}) async-start(), calls=%async_computation.3 | async-start | bytes 20480 | tf_op jit(solution)/shard_map/reduce_scatter | solution.py:39
Sparse Core Ops, SparseCore 0:
  28.3 56.1 reduce-scatter.4
  86.9 18.5 reduce-scatter.2
